TPU v7x, 32 devices: a whole 2x2x4 slice. The times are simulated.
32 devices in a mesh: groups: 2 (over x), expert: 16 (over z, y, core).
Axes of the slice: x: 2, y: 2, z: 4, core: 2. Of those that a mesh axis runs over, the one named last changes fastest.
Arguments:
- residual: bfloat16 [512, 2880], P(('groups', 'expert')), parts along dimension 0, may hold values from -6 to 6
- norm_gain: float32 [2880], replicated, may hold values from 0.1 to 1.9
- expert_ids: int32 [512, 4], P(('groups', 'expert')), parts along dimension 0, may hold values from 0 to 7, all different within a row; in each aligned block of 16 rows (0 to 15, 16 to 31, ...) at most 16 rows name the same one
- expert_weights: float32 [512, 4], P(('groups', 'expert')), parts along dimension 0, may hold values from 0.2 to 1
- gate_proj: bfloat16 [16, 2880, 720], P('expert'), may hold values from -0.109375 to 0.109375
- up_proj: bfloat16 [16, 2880, 720], P('expert'), may hold values from -0.109375 to 0.109375
- down_proj: bfloat16 [16, 720, 2880], P('expert'), may hold values from -0.15625 to 0.15625
Outputs:
- mixed: bfloat16 [512, 2880], P(('groups', 'expert')), parts along dimension 0
There are 2 independent parts, one for each index of `groups`. A program takes and returns all parts, laid end to end along the dimension named above; an argument that names none is the same for every part. Nothing has to cross between parts.
Inputs may be any that keep to these rules, and one draw needn't show every extreme that they name: `expert_ids`: in each aligned block of 16 rows (the rows of one device) no expert is named by more than 16 entries.
All inputs are finite; a program needn't handle non-finite values.
Results may differ from a plain program's by a relative error of at most 0.0063.
Values may be sent and summed in bfloat16 or wider, within the bound.
A program may use at most 64 MiB of HBM per device.

v0:
```python
import jax
import jax.numpy as jnp
from jax import lax
from jax.sharding import PartitionSpec as P


def partner(value, axis, bit):
    mask = 2**bit
    pairs = [(source, source ^ mask) for source in range(lax.axis_size(axis))]
    return lax.ppermute(value, axis, pairs)


def expert_half(block, gate_w, up_w, down_w):
    flat = block.reshape(-1, block.shape[-1])
    gate = jnp.dot(flat, gate_w, preferred_element_type=jnp.float32)
    upper = jnp.dot(flat, up_w, preferred_element_type=jnp.float32)
    act = (gate * jax.nn.sigmoid(1.702 * gate) * (upper + 1.0)).astype(jnp.bfloat16)
    out = jnp.dot(act, down_w, preferred_element_type=jnp.float32).astype(jnp.bfloat16)
    return out.reshape(block.shape[:-1] + (down_w.shape[1],))


def body(residual, norm_gain, expert_ids, expert_weights, gate_proj, up_proj, down_proj):
    rows, model = residual.shape
    chosen = expert_ids.shape[1]
    devices = lax.axis_size("expert")
    experts = devices // 2
    capacity = 2 * rows * chosen // experts
    half_cap = capacity // 2
    gate_w, up_w, down_w = (gate_proj[0], up_proj[0], down_proj[0])
    x = residual.astype(jnp.float32)
    scale = lax.rsqrt(jnp.mean(x * x, axis=-1, keepdims=True) + 1e-05)
    normed = (x * scale * norm_gain).astype(jnp.bfloat16)
    flat_ids = expert_ids.reshape(rows * chosen)
    onehot = (
        flat_ids[:, None] == lax.broadcasted_iota(jnp.int32, (rows * chosen, experts), 1)
    ).astype(jnp.int32)
    slot = jnp.sum(onehot * jnp.cumsum(onehot, axis=0), axis=1) - 1
    position = flat_ids * capacity + slot
    pick = (
        position[:, None] == lax.broadcasted_iota(jnp.int32, (rows * chosen, experts * capacity), 1)
    ).astype(jnp.float32)
    place_rows = jnp.sum(pick.reshape(rows, chosen, experts * capacity), axis=1)
    send = lax.dot_general(
        place_rows.astype(jnp.bfloat16),
        normed,
        (((0,), (0,)), ((), ())),
        preferred_element_type=jnp.float32,
    )
    send = send.astype(jnp.bfloat16).reshape(experts, capacity, model)
    outgoing = send.reshape(experts, 2, half_cap, model).reshape(devices, half_cap, model)
    arrived = lax.all_to_all(outgoing, "expert", split_axis=0, concat_axis=0, tiled=True)
    other = partner(arrived, "expert", 0)
    both = expert_half(jnp.stack((arrived, other)), gate_w, up_w, down_w)
    returned = partner(both[1], "expert", 0)
    finished = (both[0].astype(jnp.float32) + returned.astype(jnp.float32)).astype(jnp.bfloat16)
    back = lax.all_to_all(finished, "expert", split_axis=0, concat_axis=0, tiled=True)
    results = back.reshape(experts, capacity, model)
    weighted = jnp.sum(
        (pick * expert_weights.reshape(rows * chosen)[:, None]).reshape(
            rows, chosen, experts * capacity
        ),
        axis=1,
    )
    combined = jnp.dot(
        weighted,
        results.reshape(experts * capacity, model).astype(jnp.float32),
        precision=lax.Precision.HIGHEST,
    )
    return (x + combined).astype(jnp.bfloat16)


def solution(mesh):
    in_specs = (
        P(("groups", "expert"), None),
        P(),
        P(("groups", "expert"), None),
        P(("groups", "expert"), None),
        P("expert", None, None),
        P("expert", None, None),
        P("expert", None, None),
    )
    out_specs = P(("groups", "expert"), None)
    return jax.shard_map(body, mesh=mesh, in_specs=in_specs, out_specs=out_specs, check_vma=False)
```

profile of v0, /device:TPU:1, one launch (start us, length us, event | category | flops | bytes accessed | tf_op | source)
XLA Modules:
  0.0 77.1 jit_solution(909006792527382461)
XLA Ops:
  0.0 0.8 copy.23
  0.8 0.1 eq.20
  0.8 0.1 fusion.27
  0.9 0.1 reduce_window_sum.11
  1.0 0.2 select_reduce_fusion.1
  1.2 0.1 sub.7
  1.3 0.1 copy.24
  1.4 0.7 multiply_add_fusion
  2.1 1.0 %fusion.21 = f32[16]{0:T(128)S(1)} fusion(bf16[16,2880]{1,0:T(8,128)(2,1)} %param.7), kind=kLoop, calls=%fused_computation.21 | loop fusion | flops 138224 | bytes 92224 | tf_op jit(solution)/shard_map/reduce_sum | solution.py:31
  3.1 0.8 convert_reduce_fusion
  3.9 1.4 %convolution_convert_fusion = bf16[128,2880]{0,1:T(8,128)(2,1)S(1)} fusion(bf16[16,2880]{1,0:T(8,128)(2,1)} %param.7, f32[2880]{0:T(1024)} %param.8, f32[16]{0:T(128)S(1)} %add_rsqrt_fusion, bf16[16,128]{1,0:T(8,128)(2,1)S(1)} %get-tuple-element.5), kind=kOutput, calls=%fused_computation.7 | convolution fusion | flops 12349440 | bytes 845120 | tf_op jit(solution)/shard_map/dot_general | solution.py:43
  5.3 0.4 copy.25
  5.7 0.0 copy-start.1
  5.7 27.4 %all_to_all.10 = bf16[16,8,2880]{2,1,0:T(8,128)(2,1)S(1)} all-to-all(bf16[16,8,2880]{2,1,0:T(8,128)(2,1)S(1)} %bitcast.34), channel_id=1, replica_groups=mesh['groups'=2,'expert'=16] {'expert'}, dimensions={0} | all-to-all | bytes 1474560 | tf_op jit(solution)/shard_map/all_to_all | solution.py:51
  33.1 0.0 collective-permute-start
  33.1 2.2 %collective-permute-done = bf16[16,8,2880]{2,1,0:T(8,128)(2,1)S(1)} collective-permute-done((bf16[16,8,2880]{2,1,0:T(8,128)(2,1)S(1)}, bf16[16,8,2880]{2,1,0:T(8,128)(2,1)S(1)}, u32[]{:S(2)}, u32[]{:S(2)}) %collective-permute-start) | collective-permute-done | bytes 737312 | tf_op jit(solution)/shard_map/ppermute | solution.py:10
  35.3 0.2 pad_maximum_fusion
  35.5 0.0 copy-done.1
  35.5 1.3 %fusion.4 = f32[256,720]{0,1:T(8,128)S(1)} fusion(bf16[256,2880]{1,0:T(8,128)(2,1)S(1)} %bitcast.35, bf16[1,2880,720]{1,2,0:T(8,128)(2,1)S(1)} %copy-done.1), kind=kOutput, calls=%fused_computation.4 | convolution fusion | flops 1061683200 | bytes 6359040 | tf_op jit(solution)/shard_map/dot_general | solution.py:15
  36.8 9.4 %fusion.6 = bf16[256,2880]{0,1:T(8,128)(2,1)} fusion(bf16[1,720,2880]{2,1,0:T(8,128)(2,1)} %param.13, f32[256,720]{0,1:T(8,128)S(1)} %fusion.4, bf16[256,2880]{1,0:T(8,128)(2,1)S(1)} %bitcast.36, bf16[1,2880,720]{1,2,0:T(8,128)(2,1)} %param.12), kind=kOutput, calls=%fused_computation.6 | convolution fusion | flops 2125578240 | bytes 11980800 | tf_op jit(solution)/shard_map/dot_general | solution.py:18
  46.2 1.5 %fusion.31 = (bf16[128,2880]{0,1:T(8,128)(2,1)S(1)}, f32[128,2880]{0,1:T(8,128)S(1)}) fusion(bf16[256,2880]{0,1:T(8,128)(2,1)} %fusion.6), kind=kLoop, calls=%fused_computation.38 | loop fusion | flops 368640 | bytes 3686400 | tf_op jit(solution)/shard_map/slice | solution.py:54
  47.7 1.2 %copy.27 = bf16[128,2880]{1,0:T(8,128)(2,1)} copy(bf16[128,2880]{0,1:T(8,128)(2,1)S(1)} %get-tuple-element.7) | data formatting | bytes 1474560 | tf_op jit(solution)/shard_map/slice | solution.py:54
  48.9 0.1 collective-permute-start.1
  49.0 0.5 copy.26
  49.5 2.0 %collective-permute-done.1 = bf16[16,8,2880]{2,1,0:T(8,128)(2,1)} collective-permute-done((bf16[16,8,2880]{2,1,0:T(8,128)(2,1)}, bf16[16,8,2880]{2,1,0:T(8,128)(2,1)}, u32[]{:S(2)}, u32[]{:S(2)}) %collective-permute-start.1) | collective-permute-done | bytes 737312 | tf_op jit(solution)/shard_map/ppermute | solution.py:10
  51.5 1.3 %fusion.10 = bf16[16,8,2880]{2,1,0:T(8,128)(2,1)S(1)} fusion(f32[128,2880]{1,0:T(8,128)S(1)} %copy.26, bf16[16,8,2880]{2,1,0:T(8,128)(2,1)} %collective-permute-done.1), kind=kLoop, calls=%fused_computation.12 | loop fusion | flops 1105920 | bytes 2949120 | tf_op jit(solution)/shard_map/convert_element_type | solution.py:55
  52.8 0.0 copy-start
  52.8 23.3 %all_to_all.11 = bf16[16,8,2880]{2,1,0:T(8,128)(2,1)S(1)} all-to-all(bf16[16,8,2880]{2,1,0:T(8,128)(2,1)S(1)} %fusion.10), channel_id=1, replica_groups=mesh['groups'=2,'expert'=16] {'expert'}, dimensions={0} | all-to-all | bytes 1474560 | tf_op jit(solution)/shard_map/all_to_all | solution.py:56
  76.1 0.0 copy-done
  76.1 1.1 %fusion.9 = bf16[16,2880]{1,0:T(8,128)(2,1)} fusion(f32[16,128]{1,0:T(8,128)S(1)} %get-tuple-element.6, bf16[16,8,2880]{2,1,0:T(8,128)(2,1)S(1)} %all_to_all.11, bf16[16,2880]{1,0:T(8,128)(2,1)S(1)} %copy-done), kind=kOutput, calls=%fused_computation.9 | convolution fusion | flops 70917120 | bytes 929792 | tf_op jit(solution)/shard_map/dot_general | solution.py:64
  (2 shorter events, 0.0 us)
Async XLA Ops:
  5.7 29.8 %copy-start.1 = (bf16[1,2880,720]{1,2,0:T(8,128)(2,1)S(1)}, bf16[1,2880,720]{1,2,0:T(8,128)(2,1)}, u32[]{:S(2)}) copy-start(bf16[1,2880,720]{1,2,0:T(8,128)(2,1)} %param.11) | copy-start | bytes 12441604
  33.1 2.2 %collective-permute-start = (bf16[16,8,2880]{2,1,0:T(8,128)(2,1)S(1)}, bf16[16,8,2880]{2,1,0:T(8,128)(2,1)S(1)}, u32[]{:S(2)}, u32[]{:S(2)}) collective-permute-start(bf16[16,8,2880]{2,1,0:T(8,128)(2,1)S(1)} %all_to_all.10), channel_id=1, source_target_pairs={{0,1},{1,0},{2,3},{3,2},{4,5},{5,4},{6,7},{7,6},{8,9},{9,8},{10,11... | collective-permute-start | bytes 2211848 | tf_op jit(solution)/shard_map/ppermute | solution.py:10
  48.9 2.6 %collective-permute-start.1 = (bf16[16,8,2880]{2,1,0:T(8,128)(2,1)}, bf16[16,8,2880]{2,1,0:T(8,128)(2,1)}, u32[]{:S(2)}, u32[]{:S(2)}) collective-permute-start(bf16[16,8,2880]{2,1,0:T(8,128)(2,1)} %bitcast.8), channel_id=1, source_target_pairs={{0,1},{1,0},{2,3},{3,2},{4,5},{5,4},{6,7},{7,6},{8,9},{9,8},{10,11... | collective-permute-start | bytes 2211848 | tf_op jit(solution)/shard_map/ppermute | solution.py:10
  52.8 23.3 %copy-start = (bf16[16,2880]{1,0:T(8,128)(2,1)S(1)}, bf16[16,2880]{1,0:T(8,128)(2,1)}, u32[]{:S(2)}) copy-start(bf16[16,2880]{1,0:T(8,128)(2,1)} %param.7) | copy-start | bytes 276484
where the time goes:
time: 77.5 us; the launch traced here: 77.1 us
  blocking collectives  50.7 us (65%)
  matrix products  13.2 us (17%)
  other arithmetic  5.79 us (7%)
  waiting for transfers between devices  4.22 us (5%)
  local copies, waits for them, and re-layouts  3.03 us (4%)
    all_to_all x1, blocking collectives, body(): lax.all_to_all(outgoing, 'expert', split_axis=0, concat_axis=0, tiled=True)  27.4 us
    all_to_all x1, blocking collectives, body(): lax.all_to_all(finished, 'expert', split_axis=0, concat_axis=0, tiled=True)  23.3 us
    dot_general x1, matrix products, expert_half(): jnp.dot(act, down_w, preferred_element_type=jnp.float32)  9.39 us
    ppermute x2, waiting for transfers between devices, partner(): return lax.ppermute(value, axis, pairs)  4.22 us
  transfers between devices with their start and end apart: 2, of which 2 were waited for; matrix products, arithmetic and copies ran while one was open for 1% of the time, Pallas kernels for 0%

commit v1 on v0

--- a/solution.py
+++ b/solution.py
@@ -2,6 +2,28 @@
 import jax.numpy as jnp
 from jax import lax
 from jax.sharding import PartitionSpec as P
+
+
+def in_blocks(x, dim, peers):
+    before, after = (x.shape[:dim], x.shape[dim + 1 :])
+    return jnp.moveaxis(x.reshape(*before, peers, -1, *after), dim, 0)
+
+
+def laid_out(blocks, dim):
+    blocks = jnp.moveaxis(blocks, 0, dim)
+    lengths = blocks.shape
+    return blocks.reshape(*lengths[:dim], lengths[dim] * lengths[dim + 1], *lengths[dim + 2 :])
+
+
+def rotated_exchange(shard, axis, split_dim, concat_dim):
+    peers, here = (lax.axis_size(axis), lax.axis_index(axis))
+    pieces = in_blocks(shard, split_dim, peers)
+    finished = [pieces[here]]
+    for hop in range(1, peers):
+        sent = pieces[(here + hop) % peers]
+        finished.append(lax.ppermute(sent, axis, [(i, (i + hop) % peers) for i in range(peers)]))
+    pieces = jnp.stack(finished)[(here - jnp.arange(peers)) % peers]
+    return laid_out(pieces, concat_dim)
 
 
 def partner(value, axis, bit):
@@ -48,7 +70,7 @@
     )
     send = send.astype(jnp.bfloat16).reshape(experts, capacity, model)
     outgoing = send.reshape(experts, 2, half_cap, model).reshape(devices, half_cap, model)
-    arrived = lax.all_to_all(outgoing, "expert", split_axis=0, concat_axis=0, tiled=True)
+    arrived = rotated_exchange(outgoing, "expert", 0, 0)
     other = partner(arrived, "expert", 0)
     both = expert_half(jnp.stack((arrived, other)), gate_w, up_w, down_w)
     returned = partner(both[1], "expert", 0)

time: 77.5 us -> 83.3 us (1.075)
  blocking collectives: 50.7 us -> 26 us
  starting transfers between devices: 0.13 us -> 24.3 us
  waiting for transfers between devices: 4.22 us -> 7.2 us
  matrix products: 13.2 us -> 15.4 us
  local copies, waits for them, and re-layouts: 3.03 us -> 3.95 us
    all_to_all x1 -> x0, blocking collectives: 27.4 us -> none  [body(): lax.all_to_all(outgoing, 'expert', split_axis=0, concat_axis=0, tiled=True)]
    ppermute x0 -> x15, starting transfers between devices: none -> 23.7 us  [rotated_exchange(): lax.ppermute(sent, axis, [(i, (i + hop) % peers) for i in range(peers)])]
    ppermute x0 -> x15, waiting for transfers between devices: none -> 3.42 us  [rotated_exchange(): lax.ppermute(sent, axis, [(i, (i + hop) % peers) for i in range(peers)])]
    all_to_all x1, blocking collectives: 23.3 us -> 26 us  [body(): lax.all_to_all(finished, 'expert', split_axis=0, concat_axis=0, tiled=True)]
    dot_general x1, matrix products: 1.35 us -> 3.54 us  [expert_half(): gate = jnp.dot(flat, gate_w, preferred_element_type=jnp.float32)]
  transfers between devices with their start and end apart: 2 -> 17, of which waited for: 2 -> 5; matrix products, arithmetic and copies ran while one was open for 1% -> 1% of each run, Pallas kernels for 0% -> 0%
where the time goes in v1:
time: 83.3 us; the launch traced here: 82.9 us
  blocking collectives  26 us (31%)
  starting transfers between devices  24.3 us (29%)
  matrix products  15.4 us (18%)
  waiting for transfers between devices  7.2 us (9%)
  other arithmetic  5.82 us (7%)
  local copies, waits for them, and re-layouts  3.95 us (5%)
    all_to_all x1, blocking collectives, body(): lax.all_to_all(finished, 'expert', split_axis=0, concat_axis=0, tiled=True)  26 us
    ppermute x15, starting transfers between devices, rotated_exchange(): lax.ppermute(sent, axis, [(i, (i + hop) % peers) for i in range(peers)])  23.7 us
    dot_general x1, matrix products, expert_half(): jnp.dot(act, down_w, preferred_element_type=jnp.float32)  9.39 us
    ppermute x2, waiting for transfers between devices, partner(): return lax.ppermute(value, axis, pairs)  3.78 us
    dot_general x1, matrix products, expert_half(): gate = jnp.dot(flat, gate_w, preferred_element_type=jnp.float32)  3.54 us
    ppermute x15, waiting for transfers between devices, rotated_exchange(): lax.ppermute(sent, axis, [(i, (i + hop) % peers) for i in range(peers)])  3.42 us
  transfers between devices with their start and end apart: 17, of which 5 were waited for; matrix products, arithmetic and copies ran while one was open for 1% of the time, Pallas kernels for 0%

profile of v1, /device:TPU:1, one launch (start us, length us, event | category | flops | bytes accessed | tf_op | source)
XLA Modules:
  0.0 82.9 jit_solution(3718634497645402264)
XLA Ops:
  0.0 0.8 copy.53
  0.8 0.1 eq.38
  0.8 0.1 fusion.27
  0.9 0.1 reduce_window_sum.11
  1.0 0.2 select_reduce_fusion.1
  1.2 0.1 sub.20
  1.3 0.1 copy.54
  1.4 0.7 multiply_add_fusion
  2.1 1.0 %fusion.21 = f32[16]{0:T(128)S(1)} fusion(bf16[16,2880]{1,0:T(8,128)(2,1)} %param.7), kind=kLoop, calls=%fused_computation.22 | loop fusion | flops 138224 | bytes 92224 | tf_op jit(solution)/shard_map/reduce_sum | solution.py:53
  3.1 0.8 convert_reduce_fusion
  3.9 1.4 %convolution_convert_fusion = bf16[128,2880]{0,1:T(8,128)(2,1)S(1)} fusion(bf16[16,2880]{1,0:T(8,128)(2,1)} %param.7, f32[2880]{0:T(1024)} %param.8, f32[16]{0:T(128)S(1)} %add_rsqrt_fusion, bf16[16,128]{1,0:T(8,128)(2,1)S(1)} %get-tuple-element.5), kind=kOutput, calls=%fused_computation.8 | convolution fusion | flops 12349440 | bytes 845120 | tf_op jit(solution)/shard_map/dot_general | solution.py:65
  5.3 0.4 copy.55
  5.7 0.1 dynamic-slice_bitcast_fusion
  5.9 2.7 %collective-permute-start = (bf16[1,8,2880]{2,1,0:T(8,128)(2,1)S(1)}, bf16[1,8,2880]{2,1,0:T(8,128)(2,1)S(1)}, u32[]{:S(2)}, u32[]{:S(2)}) collective-permute-start(bf16[1,8,2880]{2,1,0:T(8,128)(2,1)S(1)} %get-tuple-element.23), channel_id=1, source_target_pairs={{0,1},{1,2},{2,3},{3,4},{4,5},{5,6},{6,7},{7,8},{8,9},{9,10},{10,1... | collective-permute-start | bytes 138248 | tf_op jit(solution)/shard_map/ppermute | solution.py:24
  8.5 1.2 %collective-permute-start.1 = (bf16[1,8,2880]{2,1,0:T(8,128)(2,1)S(1)}, bf16[1,8,2880]{2,1,0:T(8,128)(2,1)S(1)}, u32[]{:S(2)}, u32[]{:S(2)}) collective-permute-start(bf16[1,8,2880]{2,1,0:T(8,128)(2,1)S(1)} %get-tuple-element.22), channel_id=1, source_target_pairs={{0,2},{1,3},{2,4},{3,5},{4,6},{5,7},{6,8},{7,9},{8,10},{9,11},{10,... | collective-permute-start | bytes 138248 | tf_op jit(solution)/shard_map/ppermute | solution.py:24
  9.8 0.4 collective-permute-start.2
  10.2 1.3 %collective-permute-start.3 = (bf16[1,8,2880]{2,1,0:T(8,128)(2,1)S(1)}, bf16[1,8,2880]{2,1,0:T(8,128)(2,1)S(1)}, u32[]{:S(2)}, u32[]{:S(2)}) collective-permute-start(bf16[1,8,2880]{2,1,0:T(8,128)(2,1)S(1)} %get-tuple-element.20), channel_id=1, source_target_pairs={{0,4},{1,5},{2,6},{3,7},{4,8},{5,9},{6,10},{7,11},{8,12},{9,13},{1... | collective-permute-start | bytes 138248 | tf_op jit(solution)/shard_map/ppermute | solution.py:24
  11.5 2.4 %collective-permute-start.4 = (bf16[1,8,2880]{2,1,0:T(8,128)(2,1)S(1)}, bf16[1,8,2880]{2,1,0:T(8,128)(2,1)S(1)}, u32[]{:S(2)}, u32[]{:S(2)}) collective-permute-start(bf16[1,8,2880]{2,1,0:T(8,128)(2,1)S(1)} %get-tuple-element.19), channel_id=1, source_target_pairs={{0,5},{1,6},{2,7},{3,8},{4,9},{5,10},{6,11},{7,12},{8,13},{9,14},{... | collective-permute-start | bytes 138248 | tf_op jit(solution)/shard_map/ppermute | solution.py:24
  13.9 0.0 collective-permute-done
  13.9 2.2 %collective-permute-start.5 = (bf16[1,8,2880]{2,1,0:T(8,128)(2,1)S(1)}, bf16[1,8,2880]{2,1,0:T(8,128)(2,1)S(1)}, u32[]{:S(2)}, u32[]{:S(2)}) collective-permute-start(bf16[1,8,2880]{2,1,0:T(8,128)(2,1)S(1)} %get-tuple-element.18), channel_id=1, source_target_pairs={{0,6},{1,7},{2,8},{3,9},{4,10},{5,11},{6,12},{7,13},{8,14},{9,15},... | collective-permute-start | bytes 138248 | tf_op jit(solution)/shard_map/ppermute | solution.py:24
  16.1 0.0 collective-permute-done.1
  16.1 0.6 collective-permute-start.6
  16.7 0.0 collective-permute-done.2
  16.7 1.0 %collective-permute-start.7 = (bf16[1,8,2880]{2,1,0:T(8,128)(2,1)S(1)}, bf16[1,8,2880]{2,1,0:T(8,128)(2,1)S(1)}, u32[]{:S(2)}, u32[]{:S(2)}) collective-permute-start(bf16[1,8,2880]{2,1,0:T(8,128)(2,1)S(1)} %get-tuple-element.16), channel_id=1, source_target_pairs={{0,8},{1,9},{2,10},{3,11},{4,12},{5,13},{6,14},{7,15},{8,0},{9,1},... | collective-permute-start | bytes 138248 | tf_op jit(solution)/shard_map/ppermute | solution.py:24
  17.7 0.0 collective-permute-done.3
  17.7 3.8 %collective-permute-start.8 = (bf16[1,8,2880]{2,1,0:T(8,128)(2,1)S(1)}, bf16[1,8,2880]{2,1,0:T(8,128)(2,1)S(1)}, u32[]{:S(2)}, u32[]{:S(2)}) collective-permute-start(bf16[1,8,2880]{2,1,0:T(8,128)(2,1)S(1)} %get-tuple-element.15), channel_id=1, source_target_pairs={{0,9},{1,10},{2,11},{3,12},{4,13},{5,14},{6,15},{7,0},{8,1},{9,2},... | collective-permute-start | bytes 138248 | tf_op jit(solution)/shard_map/ppermute | solution.py:24
  21.6 0.0 collective-permute-done.4
  21.6 2.0 %collective-permute-start.9 = (bf16[1,8,2880]{2,1,0:T(8,128)(2,1)S(1)}, bf16[1,8,2880]{2,1,0:T(8,128)(2,1)S(1)}, u32[]{:S(2)}, u32[]{:S(2)}) collective-permute-start(bf16[1,8,2880]{2,1,0:T(8,128)(2,1)S(1)} %get-tuple-element.14), channel_id=1, source_target_pairs={{0,10},{1,11},{2,12},{3,13},{4,14},{5,15},{6,0},{7,1},{8,2},{9,3},... | collective-permute-start | bytes 138248 | tf_op jit(solution)/shard_map/ppermute | solution.py:24
  23.5 0.0 collective-permute-done.5
  23.5 0.2 collective-permute-start.10
  23.7 0.0 collective-permute-done.6
  23.7 0.7 collective-permute-start.11
  24.4 0.0 collective-permute-done.7
  24.5 3.6 %collective-permute-start.12 = (bf16[1,8,2880]{2,1,0:T(8,128)(2,1)S(1)}, bf16[1,8,2880]{2,1,0:T(8,128)(2,1)S(1)}, u32[]{:S(2)}, u32[]{:S(2)}) collective-permute-start(bf16[1,8,2880]{2,1,0:T(8,128)(2,1)S(1)} %get-tuple-element.11), channel_id=1, source_target_pairs={{0,13},{1,14},{2,15},{3,0},{4,1},{5,2},{6,3},{7,4},{8,5},{9,6},{10... | collective-permute-start | bytes 138248 | tf_op jit(solution)/shard_map/ppermute | solution.py:24
  28.1 0.0 collective-permute-done.8
  28.1 1.6 %collective-permute-start.13 = (bf16[1,8,2880]{2,1,0:T(8,128)(2,1)S(1)}, bf16[1,8,2880]{2,1,0:T(8,128)(2,1)S(1)}, u32[]{:S(2)}, u32[]{:S(2)}) collective-permute-start(bf16[1,8,2880]{2,1,0:T(8,128)(2,1)S(1)} %get-tuple-element.10), channel_id=1, source_target_pairs={{0,14},{1,15},{2,0},{3,1},{4,2},{5,3},{6,4},{7,5},{8,6},{9,7},{10,... | collective-permute-start | bytes 138248 | tf_op jit(solution)/shard_map/ppermute | solution.py:24
  29.7 0.0 collective-permute-done.9
  29.7 0.1 collective-permute-start.14
  29.7 0.0 collective-permute-done.10
  29.8 0.0 collective-permute-done.11
  29.8 0.1 collective-permute-done.12
  29.9 1.2 %collective-permute-done.13 = bf16[1,8,2880]{2,1,0:T(8,128)(2,1)S(1)} collective-permute-done((bf16[1,8,2880]{2,1,0:T(8,128)(2,1)S(1)}, bf16[1,8,2880]{2,1,0:T(8,128)(2,1)S(1)}, u32[]{:S(2)}, u32[]{:S(2)}) %collective-permute-start.13) | collective-permute-done | bytes 46112 | tf_op jit(solution)/shard_map/ppermute | solution.py:24
  31.1 2.2 %collective-permute-done.14 = bf16[1,8,2880]{2,1,0:T(8,128)(2,1)S(1)} collective-permute-done((bf16[1,8,2880]{2,1,0:T(8,128)(2,1)S(1)}, bf16[1,8,2880]{2,1,0:T(8,128)(2,1)S(1)}, u32[]{:S(2)}, u32[]{:S(2)}) %collective-permute-start.14) | collective-permute-done | bytes 46112 | tf_op jit(solution)/shard_map/ppermute | solution.py:24
  33.2 0.6 gather_fusion
  33.9 0.4 collective-permute-start.15
  34.2 2.0 %collective-permute-done.15 = bf16[16,8,2880]{2,1,0:T(8,128)(2,1)S(1)} collective-permute-done((bf16[16,8,2880]{2,1,0:T(8,128)(2,1)S(1)}, bf16[16,8,2880]{2,1,0:T(8,128)(2,1)S(1)}, u32[]{:S(2)}, u32[]{:S(2)}) %collective-permute-start.15) | collective-permute-done | bytes 737312 | tf_op jit(solution)/shard_map/ppermute | solution.py:32
  36.2 0.2 pad_maximum_fusion
  36.3 3.5 %fusion.4 = f32[256,720]{0,1:T(8,128)S(1)} fusion(bf16[256,2880]{1,0:T(8,128)(2,1)S(1)} %bitcast.128, bf16[1,2880,720]{1,2,0:T(8,128)(2,1)} %param.11), kind=kOutput, calls=%fused_computation.5 | convolution fusion | flops 1061683200 | bytes 6359040 | tf_op jit(solution)/shard_map/dot_general | solution.py:37
  39.9 9.4 %fusion.6 = bf16[256,2880]{0,1:T(8,128)(2,1)} fusion(bf16[1,720,2880]{2,1,0:T(8,128)(2,1)} %param.13, f32[256,720]{0,1:T(8,128)S(1)} %fusion.4, bf16[256,2880]{1,0:T(8,128)(2,1)S(1)} %bitcast.129, bf16[1,2880,720]{1,2,0:T(8,128)(2,1)} %param.12), kind=kOutput, calls=%fused_computation.7 | convolution fusion | flops 2125578240 | bytes 11980800 | tf_op jit(solution)/shard_map/dot_general | solution.py:40
  49.3 1.5 %fusion.33 = (bf16[128,2880]{0,1:T(8,128)(2,1)S(1)}, f32[128,2880]{0,1:T(8,128)S(1)}) fusion(bf16[256,2880]{0,1:T(8,128)(2,1)} %fusion.6), kind=kLoop, calls=%fused_computation.77 | loop fusion | flops 368640 | bytes 3686400 | tf_op jit(solution)/shard_map/slice | solution.py:76
  50.8 1.2 %copy.72 = bf16[128,2880]{1,0:T(8,128)(2,1)} copy(bf16[128,2880]{0,1:T(8,128)(2,1)S(1)} %get-tuple-element.7) | data formatting | bytes 1474560 | tf_op jit(solution)/shard_map/slice | solution.py:76
  51.9 0.3 collective-permute-start.16
  52.2 0.5 copy.71
  52.7 1.8 %collective-permute-done.16 = bf16[16,8,2880]{2,1,0:T(8,128)(2,1)} collective-permute-done((bf16[16,8,2880]{2,1,0:T(8,128)(2,1)}, bf16[16,8,2880]{2,1,0:T(8,128)(2,1)}, u32[]{:S(2)}, u32[]{:S(2)}) %collective-permute-start.16) | collective-permute-done | bytes 737312 | tf_op jit(solution)/shard_map/ppermute | solution.py:32
  54.5 1.3 %fusion.10 = bf16[16,8,2880]{2,1,0:T(8,128)(2,1)S(1)} fusion(f32[128,2880]{1,0:T(8,128)S(1)} %copy.71, bf16[16,8,2880]{2,1,0:T(8,128)(2,1)} %collective-permute-done.16), kind=kLoop, calls=%fused_computation.13 | loop fusion | flops 1105920 | bytes 2949120 | tf_op jit(solution)/shard_map/convert_element_type | solution.py:77
  55.8 0.0 copy-start
  55.8 26.0 %all_to_all.5 = bf16[16,8,2880]{2,1,0:T(8,128)(2,1)S(1)} all-to-all(bf16[16,8,2880]{2,1,0:T(8,128)(2,1)S(1)} %fusion.10), channel_id=1, replica_groups=mesh['groups'=2,'expert'=16] {'expert'}, dimensions={0} | all-to-all | bytes 1474560 | tf_op jit(solution)/shard_map/all_to_all | solution.py:78
  81.8 0.0 copy-done
  81.8 1.1 %fusion.9 = bf16[16,2880]{1,0:T(8,128)(2,1)} fusion(f32[16,128]{1,0:T(8,128)S(1)} %get-tuple-element.6, bf16[16,8,2880]{2,1,0:T(8,128)(2,1)S(1)} %all_to_all.5, bf16[16,2880]{1,0:T(8,128)(2,1)S(1)} %copy-done), kind=kOutput, calls=%fused_computation.10 | convolution fusion | flops 70917120 | bytes 929792 | tf_op jit(solution)/shard_map/dot_general | solution.py:86
  (19 shorter events, 0.2 us)
Async XLA Ops:
  5.9 8.1 %collective-permute-start = (bf16[1,8,2880]{2,1,0:T(8,128)(2,1)S(1)}, bf16[1,8,2880]{2,1,0:T(8,128)(2,1)S(1)}, u32[]{:S(2)}, u32[]{:S(2)}) collective-permute-start(bf16[1,8,2880]{2,1,0:T(8,128)(2,1)S(1)} %get-tuple-element.23), channel_id=1, source_target_pairs={{0,1},{1,2},{2,3},{3,4},{4,5},{5,6},{6,7},{7,8},{8,9},{9,10},{10,1... | collective-permute-start | bytes 138248 | tf_op jit(solution)/shard_map/ppermute | solution.py:24
  8.5 7.6 %collective-permute-start.1 = (bf16[1,8,2880]{2,1,0:T(8,128)(2,1)S(1)}, bf16[1,8,2880]{2,1,0:T(8,128)(2,1)S(1)}, u32[]{:S(2)}, u32[]{:S(2)}) collective-permute-start(bf16[1,8,2880]{2,1,0:T(8,128)(2,1)S(1)} %get-tuple-element.22), channel_id=1, source_target_pairs={{0,2},{1,3},{2,4},{3,5},{4,6},{5,7},{6,8},{7,9},{8,10},{9,11},{10,... | collective-permute-start | bytes 138248 | tf_op jit(solution)/shard_map/ppermute | solution.py:24
  9.8 6.9 %collective-permute-start.2 = (bf16[1,8,2880]{2,1,0:T(8,128)(2,1)S(1)}, bf16[1,8,2880]{2,1,0:T(8,128)(2,1)S(1)}, u32[]{:S(2)}, u32[]{:S(2)}) collective-permute-start(bf16[1,8,2880]{2,1,0:T(8,128)(2,1)S(1)} %get-tuple-element.21), channel_id=1, source_target_pairs={{0,3},{1,4},{2,5},{3,6},{4,7},{5,8},{6,9},{7,10},{8,11},{9,12},{10... | collective-permute-start | bytes 138248 | tf_op jit(solution)/shard_map/ppermute | solution.py:24
  10.2 7.5 %collective-permute-start.3 = (bf16[1,8,2880]{2,1,0:T(8,128)(2,1)S(1)}, bf16[1,8,2880]{2,1,0:T(8,128)(2,1)S(1)}, u32[]{:S(2)}, u32[]{:S(2)}) collective-permute-start(bf16[1,8,2880]{2,1,0:T(8,128)(2,1)S(1)} %get-tuple-element.20), channel_id=1, source_target_pairs={{0,4},{1,5},{2,6},{3,7},{4,8},{5,9},{6,10},{7,11},{8,12},{9,13},{1... | collective-permute-start | bytes 138248 | tf_op jit(solution)/shard_map/ppermute | solution.py:24
  11.5 10.1 %collective-permute-start.4 = (bf16[1,8,2880]{2,1,0:T(8,128)(2,1)S(1)}, bf16[1,8,2880]{2,1,0:T(8,128)(2,1)S(1)}, u32[]{:S(2)}, u32[]{:S(2)}) collective-permute-start(bf16[1,8,2880]{2,1,0:T(8,128)(2,1)S(1)} %get-tuple-element.19), channel_id=1, source_target_pairs={{0,5},{1,6},{2,7},{3,8},{4,9},{5,10},{6,11},{7,12},{8,13},{9,14},{... | collective-permute-start | bytes 138248 | tf_op jit(solution)/shard_map/ppermute | solution.py:24
  13.9 9.6 %collective-permute-start.5 = (bf16[1,8,2880]{2,1,0:T(8,128)(2,1)S(1)}, bf16[1,8,2880]{2,1,0:T(8,128)(2,1)S(1)}, u32[]{:S(2)}, u32[]{:S(2)}) collective-permute-start(bf16[1,8,2880]{2,1,0:T(8,128)(2,1)S(1)} %get-tuple-element.18), channel_id=1, source_target_pairs={{0,6},{1,7},{2,8},{3,9},{4,10},{5,11},{6,12},{7,13},{8,14},{9,15},... | collective-permute-start | bytes 138248 | tf_op jit(solution)/shard_map/ppermute | solution.py:24
  16.1 7.6 %collective-permute-start.6 = (bf16[1,8,2880]{2,1,0:T(8,128)(2,1)S(1)}, bf16[1,8,2880]{2,1,0:T(8,128)(2,1)S(1)}, u32[]{:S(2)}, u32[]{:S(2)}) collective-permute-start(bf16[1,8,2880]{2,1,0:T(8,128)(2,1)S(1)} %get-tuple-element.17), channel_id=1, source_target_pairs={{0,7},{1,8},{2,9},{3,10},{4,11},{5,12},{6,13},{7,14},{8,15},{9,0},... | collective-permute-start | bytes 138248 | tf_op jit(solution)/shard_map/ppermute | solution.py:24
  16.7 7.7 %collective-permute-start.7 = (bf16[1,8,2880]{2,1,0:T(8,128)(2,1)S(1)}, bf16[1,8,2880]{2,1,0:T(8,128)(2,1)S(1)}, u32[]{:S(2)}, u32[]{:S(2)}) collective-permute-start(bf16[1,8,2880]{2,1,0:T(8,128)(2,1)S(1)} %get-tuple-element.16), channel_id=1, source_target_pairs={{0,8},{1,9},{2,10},{3,11},{4,12},{5,13},{6,14},{7,15},{8,0},{9,1},... | collective-permute-start | bytes 138248 | tf_op jit(solution)/shard_map/ppermute | solution.py:24
  17.7 10.4 %collective-permute-start.8 = (bf16[1,8,2880]{2,1,0:T(8,128)(2,1)S(1)}, bf16[1,8,2880]{2,1,0:T(8,128)(2,1)S(1)}, u32[]{:S(2)}, u32[]{:S(2)}) collective-permute-start(bf16[1,8,2880]{2,1,0:T(8,128)(2,1)S(1)} %get-tuple-element.15), channel_id=1, source_target_pairs={{0,9},{1,10},{2,11},{3,12},{4,13},{5,14},{6,15},{7,0},{8,1},{9,2},... | collective-permute-start | bytes 138248 | tf_op jit(solution)/shard_map/ppermute | solution.py:24
  21.6 8.1 %collective-permute-start.9 = (bf16[1,8,2880]{2,1,0:T(8,128)(2,1)S(1)}, bf16[1,8,2880]{2,1,0:T(8,128)(2,1)S(1)}, u32[]{:S(2)}, u32[]{:S(2)}) collective-permute-start(bf16[1,8,2880]{2,1,0:T(8,128)(2,1)S(1)} %get-tuple-element.14), channel_id=1, source_target_pairs={{0,10},{1,11},{2,12},{3,13},{4,14},{5,15},{6,0},{7,1},{8,2},{9,3},... | collective-permute-start | bytes 138248 | tf_op jit(solution)/shard_map/ppermute | solution.py:24
  23.5 6.2 %collective-permute-start.10 = (bf16[1,8,2880]{2,1,0:T(8,128)(2,1)S(1)}, bf16[1,8,2880]{2,1,0:T(8,128)(2,1)S(1)}, u32[]{:S(2)}, u32[]{:S(2)}) collective-permute-start(bf16[1,8,2880]{2,1,0:T(8,128)(2,1)S(1)} %get-tuple-element.13), channel_id=1, source_target_pairs={{0,11},{1,12},{2,13},{3,14},{4,15},{5,0},{6,1},{7,2},{8,3},{9,4},{... | collective-permute-start | bytes 138248 | tf_op jit(solution)/shard_map/ppermute | solution.py:24
  23.7 6.0 %collective-permute-start.11 = (bf16[1,8,2880]{2,1,0:T(8,128)(2,1)S(1)}, bf16[1,8,2880]{2,1,0:T(8,128)(2,1)S(1)}, u32[]{:S(2)}, u32[]{:S(2)}) collective-permute-start(bf16[1,8,2880]{2,1,0:T(8,128)(2,1)S(1)} %get-tuple-element.12), channel_id=1, source_target_pairs={{0,12},{1,13},{2,14},{3,15},{4,0},{5,1},{6,2},{7,3},{8,4},{9,5},{1... | collective-permute-start | bytes 138248 | tf_op jit(solution)/shard_map/ppermute | solution.py:24
  24.5 5.4 %collective-permute-start.12 = (bf16[1,8,2880]{2,1,0:T(8,128)(2,1)S(1)}, bf16[1,8,2880]{2,1,0:T(8,128)(2,1)S(1)}, u32[]{:S(2)}, u32[]{:S(2)}) collective-permute-start(bf16[1,8,2880]{2,1,0:T(8,128)(2,1)S(1)} %get-tuple-element.11), channel_id=1, source_target_pairs={{0,13},{1,14},{2,15},{3,0},{4,1},{5,2},{6,3},{7,4},{8,5},{9,6},{10... | collective-permute-start | bytes 138248 | tf_op jit(solution)/shard_map/ppermute | solution.py:24
  28.1 3.0 %collective-permute-start.13 = (bf16[1,8,2880]{2,1,0:T(8,128)(2,1)S(1)}, bf16[1,8,2880]{2,1,0:T(8,128)(2,1)S(1)}, u32[]{:S(2)}, u32[]{:S(2)}) collective-permute-start(bf16[1,8,2880]{2,1,0:T(8,128)(2,1)S(1)} %get-tuple-element.10), channel_id=1, source_target_pairs={{0,14},{1,15},{2,0},{3,1},{4,2},{5,3},{6,4},{7,5},{8,6},{9,7},{10,... | collective-permute-start | bytes 138248 | tf_op jit(solution)/shard_map/ppermute | solution.py:24
  29.7 3.5 %collective-permute-start.14 = (bf16[1,8,2880]{2,1,0:T(8,128)(2,1)S(1)}, bf16[1,8,2880]{2,1,0:T(8,128)(2,1)S(1)}, u32[]{:S(2)}, u32[]{:S(2)}) collective-permute-start(bf16[1,8,2880]{2,1,0:T(8,128)(2,1)S(1)} %get-tuple-element.9), channel_id=1, source_target_pairs={{0,15},{1,0},{2,1},{3,2},{4,3},{5,4},{6,5},{7,6},{8,7},{9,8},{10,9... | collective-permute-start | bytes 138248 | tf_op jit(solution)/shard_map/ppermute | solution.py:24
  33.9 2.3 %collective-permute-start.15 = (bf16[16,8,2880]{2,1,0:T(8,128)(2,1)S(1)}, bf16[16,8,2880]{2,1,0:T(8,128)(2,1)S(1)}, u32[]{:S(2)}, u32[]{:S(2)}) collective-permute-start(bf16[16,8,2880]{2,1,0:T(8,128)(2,1)S(1)} %gather_fusion), channel_id=1, source_target_pairs={{0,1},{1,0},{2,3},{3,2},{4,5},{5,4},{6,7},{7,6},{8,9},{9,8},{10,11... | collective-permute-start | bytes 2211848 | tf_op jit(solution)/shard_map/ppermute | solution.py:32
  51.9 2.6 %collective-permute-start.16 = (bf16[16,8,2880]{2,1,0:T(8,128)(2,1)}, bf16[16,8,2880]{2,1,0:T(8,128)(2,1)}, u32[]{:S(2)}, u32[]{:S(2)}) collective-permute-start(bf16[16,8,2880]{2,1,0:T(8,128)(2,1)} %bitcast.55), channel_id=1, source_target_pairs={{0,1},{1,0},{2,3},{3,2},{4,5},{5,4},{6,7},{7,6},{8,9},{9,8},{10,11... | collective-permute-start | bytes 2211848 | tf_op jit(solution)/shard_map/ppermute | solution.py:32
  55.8 26.0 %copy-start = (bf16[16,2880]{1,0:T(8,128)(2,1)S(1)}, bf16[16,2880]{1,0:T(8,128)(2,1)}, u32[]{:S(2)}) copy-start(bf16[16,2880]{1,0:T(8,128)(2,1)} %param.7) | copy-start | bytes 276484
